TPU v7x, 512 devices: a whole 4x8x8 slice. The times are simulated.
512 devices in a mesh: ctx: 64 (over y, z_lo, x), mp: 8 (over z_hi, core).
Axes of the slice: x: 4, y: 8, z: 8 (z_hi: 4, z_lo: 2; z = z_hi * 2 + z_lo), core: 2. Of those that a mesh axis runs over, the one named last changes fastest.
Arguments:
- queries: bfloat16 [16384, 8192], P('ctx', 'mp'), may hold values from -6 to 6
- key_feats: bfloat16 [16384, 8192], P('ctx', 'mp'), may hold values from -6 to 6
- value_feats: bfloat16 [16384, 8192], P('ctx', 'mp'), may hold values from -6 to 6
- filters: bfloat16 [512, 128], P('mp'), may hold values from -0.5 to 0.5
- grad_out: bfloat16 [16384, 8192], P('ctx', 'mp'), may hold values from -40 to 40
Outputs:
- mixer_out: bfloat16 [16384, 8192], P('ctx', 'mp')
- grad_queries: bfloat16 [16384, 8192], P('ctx', 'mp')
- grad_keys: bfloat16 [16384, 8192], P('ctx', 'mp')
- grad_values: bfloat16 [16384, 8192], P('ctx', 'mp')
- grad_filters: float32 [512, 128], P('mp')
All inputs are finite; a program needn't handle non-finite values.
Results may differ from a plain program's by a relative error of at most 0.0058.
Values may be sent and summed in bfloat16 or wider, within the bound.
No kernel may reach another device: no remote copies, remote signals or barrier semaphores. Data moves between devices by JAX's collectives and lax.ppermute only.
A program may use at most 64 MiB of HBM per device.

v0:
```python
import jax
import jax.numpy as jnp
from jax import lax
from jax.sharding import PartitionSpec as P

D = 8192
G = 16


def contract(formula, first_op, second_op):
    return jnp.einsum(formula, first_op, second_op, preferred_element_type=jnp.float32)


def toeplitz(filt):
    count, filter_len = filt.shape
    flipped = filt[:, ::-1]
    lead_zero = jnp.zeros((count, 1), filt.dtype)
    trailing = jnp.zeros((count, filter_len), filt.dtype)
    pattern = jnp.concatenate([lead_zero, flipped, trailing], axis=1)
    repeated = jnp.tile(pattern, (1, filter_len))
    return repeated[:, : filter_len * 2 * filter_len].reshape(count, filter_len, 2 * filter_len)


def make_windows(blocks, before):
    earlier = jnp.concatenate([before[:, :, None, :], blocks[:, :, :-1, :]], axis=2)
    return jnp.concatenate([earlier, blocks], axis=3)


def forward_conv(signal, before, toeplitz_mat):
    groups_here, group_size, seq_len = signal.shape
    filter_len = toeplitz_mat.shape[1]
    blocks = signal.reshape(groups_here, group_size, seq_len // filter_len, filter_len)
    window_rows = make_windows(blocks, before)
    result = contract("gam,gsnm->gsna", toeplitz_mat, window_rows)
    return (result.reshape(groups_here, group_size, seq_len), window_rows)


def backward_conv(grad_rows, after, toeplitz_mat):
    groups_here, group_size, seq_len = grad_rows.shape
    filter_len = toeplitz_mat.shape[1]
    blocks = grad_rows.reshape(groups_here, group_size, seq_len // filter_len, filter_len)
    spread = contract("gam,gsna->gsnm", toeplitz_mat, blocks)
    tail_part = contract("gam,gsa->gsm", toeplitz_mat, after)
    next_part = jnp.concatenate(
        [spread[:, :, 1:, :filter_len], tail_part[:, :, None, :filter_len]], axis=2
    )
    return (spread[:, :, :, filter_len:] + next_part).reshape(groups_here, group_size, seq_len)


def filter_grad(grad_rows, window_rows, filter_len):
    groups_here, group_size, seq_len = grad_rows.shape
    blocks = grad_rows.reshape(groups_here, group_size, seq_len // filter_len, filter_len)
    correlate = contract("gsna,gsnm->gam", blocks, window_rows)
    flattened = correlate.reshape(groups_here, filter_len * 2 * filter_len)
    flattened = jnp.concatenate(
        [flattened, jnp.zeros((groups_here, filter_len), jnp.float32)], axis=1
    )
    flattened = flattened.reshape(groups_here, filter_len, 2 * filter_len + 1)
    diagonals = jnp.sum(flattened, axis=1)
    return diagonals[:, 1 : filter_len + 1][:, ::-1]


def shards(queries, key_feats, value_feats, filters, grad_out):
    tokens, channels = queries.shape
    slab_groups, filter_len = filters.shape
    product = (
        (key_feats.astype(jnp.float32) * value_feats.astype(jnp.float32)).astype(jnp.bfloat16).T
    )
    grad_mix = (grad_out.astype(jnp.float32) * queries.astype(jnp.float32)).astype(jnp.bfloat16).T
    owners = lax.axis_size("ctx")
    own_width = channels // owners
    own_groups = own_width // G
    signal = lax.all_to_all(product, "ctx", split_axis=0, concat_axis=1, tiled=True)
    grad_rows = lax.all_to_all(grad_mix, "ctx", split_axis=0, concat_axis=1, tiled=True)
    seq_len = signal.shape[1]
    signal = signal.reshape(own_groups, G, seq_len)
    grad_rows = grad_rows.reshape(own_groups, G, seq_len)
    first_group = lax.axis_index("ctx") * own_groups
    own_filters = lax.dynamic_slice_in_dim(filters, first_group, own_groups, 0)
    toeplitz_mat = toeplitz(own_filters)
    zero_rim = jnp.zeros((own_groups, G, filter_len), jnp.bfloat16)
    conv_out, window_rows = forward_conv(signal, zero_rim, toeplitz_mat)
    conv_out = conv_out.astype(jnp.bfloat16).reshape(own_width, seq_len)
    conv_grad = (
        backward_conv(grad_rows, zero_rim, toeplitz_mat)
        .astype(jnp.bfloat16)
        .reshape(own_width, seq_len)
    )
    partial_grad = filter_grad(grad_rows, window_rows, filter_len)
    conv_rows = lax.all_to_all(conv_out, "ctx", split_axis=1, concat_axis=0, tiled=True)
    grad_back = lax.all_to_all(conv_grad, "ctx", split_axis=1, concat_axis=0, tiled=True)
    raw_filters = lax.all_gather(partial_grad, "ctx", axis=0, tiled=True)
    conv_f = conv_rows.T.astype(jnp.float32)
    back_f = grad_back.T.astype(jnp.float32)
    mixer_out = (queries.astype(jnp.float32) * conv_f).astype(jnp.bfloat16)
    grad_queries = (grad_out.astype(jnp.float32) * conv_f).astype(jnp.bfloat16)
    grad_keys = (back_f * value_feats.astype(jnp.float32)).astype(jnp.bfloat16)
    grad_values = (back_f * key_feats.astype(jnp.float32)).astype(jnp.bfloat16)
    square_sum = lax.psum(jnp.sum(raw_filters * raw_filters), "mp")
    grad_rms = jnp.sqrt(square_sum / (D // G * filter_len) + 1e-06)
    grad_filters = raw_filters * jnp.minimum(1.0, 1.0 / grad_rms)
    return (mixer_out, grad_queries, grad_keys, grad_values, grad_filters)


def solution(mesh):
    placed = (P("ctx", "mp"), P("ctx", "mp"), P("ctx", "mp"), P("mp", None), P("ctx", "mp"))
    return jax.shard_map(
        shards,
        mesh=mesh,
        in_specs=placed,
        out_specs=(P("ctx", "mp"), P("ctx", "mp"), P("ctx", "mp"), P("ctx", "mp"), P("mp", None)),
        check_vma=False,
    )
```

profile of v0, /device:TPU:1, one launch (start us, length us, event | category | flops | bytes accessed | tf_op | source)
XLA Modules:
  0.0 278.9 jit_solution(11719873778474944530)
XLA Ops:
  0.6 0.0 copy-start
  0.6 1.2 copy.28
  1.9 1.2 copy.33
  3.1 0.9 fusion.6
  4.1 12.9 %all-to-all-start.2 = ((bf16[64,16,256]{2,1,0:T(8,128)(2,1)}), bf16[64,16,256]{2,1,0:T(8,128)(2,1)S(1)}, u32[]{:S(2)}, u32[]{:S(2)}) async-start(bf16[64,16,256]{2,1,0:T(8,128)(2,1)} %bitcast.10), calls=%async_computation.2 | async-start | bytes 1048576 | tf_op jit(solution)/shard_map/all_to_all | solution.py:74
  17.0 0.1 rev.6
  17.1 0.1 pad.6.clone
  17.2 0.1 fusion.13
  17.3 0.4 tile.13
  17.7 0.4 slice_reduce_fusion
  18.2 0.1 convolution_bitcast_fusion.2
  18.3 14.5 %all-to-all-done.2 = bf16[64,16,256]{2,1,0:T(8,128)(2,1)S(1)} async-done(((bf16[64,16,256]{2,1,0:T(8,128)(2,1)}), bf16[64,16,256]{2,1,0:T(8,128)(2,1)S(1)}, u32[]{:S(2)}, u32[]{:S(2)}) %all-to-all-start.2) | async-done | bytes 524320 | tf_op jit(solution)/shard_map/all_to_all | solution.py:74
  32.8 0.2 copy.34
  32.9 0.2 reshape.85
  33.1 0.4 convolution_bitcast_fusion
  33.5 0.1 slice.27
  33.6 0.1 fusion.9
  33.8 0.0 copy-start.1
  33.8 0.2 convert_element_type.93
  34.0 1.1 copy.35
  35.0 7.2 %all-to-all-start.3 = ((bf16[16,64,256]{2,0,1:T(8,128)(2,1)}), bf16[16,64,256]{2,0,1:T(8,128)(2,1)S(1)}, u32[]{:S(2)}, u32[]{:S(2)}) async-start(bf16[16,64,256]{2,0,1:T(8,128)(2,1)} %copy.35), calls=%async_computation.3 | async-start | bytes 1048576 | tf_op jit(solution)/shard_map/all_to_all | solution.py:91
  42.2 1.0 copy.29
  43.2 1.0 copy.30
  44.2 12.8 %all-to-all-done.3 = bf16[16,64,256]{2,0,1:T(8,128)(2,1)S(1)} async-done(((bf16[16,64,256]{2,0,1:T(8,128)(2,1)}), bf16[16,64,256]{2,0,1:T(8,128)(2,1)S(1)}, u32[]{:S(2)}, u32[]{:S(2)}) %all-to-all-start.3) | async-done | bytes 524320 | tf_op jit(solution)/shard_map/all_to_all | solution.py:91
  57.0 1.5 fusion.2
  58.5 21.8 %all_to_all.52 = bf16[64,16,256]{2,1,0:T(8,128)(2,1)S(1)} all-to-all(bf16[64,16,256]{2,1,0:T(8,128)(2,1)S(1)} %bitcast.50), channel_id=1, replica_groups=mesh['ctx'=64,'mp'=8] {'ctx'}, dimensions={0} | all-to-all | bytes 1048576 | tf_op jit(solution)/shard_map/all_to_all | solution.py:73
  80.4 0.2 copy.31
  80.5 1.0 reshape_reshape.2
  81.5 2.4 convolution_convert_fusion
  83.9 1.2 convert_element_type.83
  85.1 1.1 copy.32
  86.2 8.1 %all-to-all-start.1 = ((bf16[16,64,256]{2,0,1:T(8,128)(2,1)}), bf16[16,64,256]{2,0,1:T(8,128)(2,1)S(1)}, u32[]{:S(2)}, u32[]{:S(2)}) async-start(bf16[16,64,256]{2,0,1:T(8,128)(2,1)} %copy.32), calls=%async_computation.1 | async-start | bytes 1048576 | tf_op jit(solution)/shard_map/all_to_all | solution.py:90
  94.4 1.0 copy.39
  95.4 1.5 convolution_bitcast_fusion.1
  96.9 0.1 copy.42
  97.1 0.3 pad_reduce_fusion
  97.4 0.3 reshape.87
  97.8 0.1 slice.29
  97.8 0.1 rev.7
  97.9 127.5 %all-gather = f32[64,1,128]{2,1,0:T(1,128)S(1)} all-gather(f32[1,1,128]{2,1,0:T(1,128)S(1)} %bitcast.57), channel_id=1, replica_groups=mesh['ctx'=64,'mp'=8] {'ctx'}, dimensions={0}, use_global_device_ids=true | all-gather | bytes 33280 | tf_op jit(solution)/shard_map/all_gather | solution.py:92
  225.5 0.7 multiply_reduce_fusion
  226.1 1.0 copy.40
  227.1 48.2 %psum.7 = f32[]{:T(128)} all-reduce(f32[]{:T(128)} %multiply_reduce_fusion), channel_id=1, replica_groups=mesh['ctx'=64,'mp'=8] {'mp'}, use_global_device_ids=true, to_apply=%region_2.0 | all-reduce | flops 1 | bytes 8 | tf_op jit(solution)/shard_map/psum | solution.py:99
  276.0 0.6 broadcast_multiply_fusion
  276.6 0.0 all-to-all-done.1
  276.6 0.2 fusion.5
  276.9 1.0 copy.37
  277.9 1.0 copy.38
  (12 shorter events, 0.1 us)
Async XLA Ops:
  0.6 16.4 %copy-start = (bf16[64,128]{1,0:T(8,128)(2,1)S(1)}, bf16[64,128]{1,0:T(8,128)(2,1)}, u32[]{:S(2)}) copy-start(bf16[64,128]{1,0:T(8,128)(2,1)} %param.8) | copy-start | bytes 49156
  4.1 28.7 %all-to-all-start.2 = ((bf16[64,16,256]{2,1,0:T(8,128)(2,1)}), bf16[64,16,256]{2,1,0:T(8,128)(2,1)S(1)}, u32[]{:S(2)}, u32[]{:S(2)}) async-start(bf16[64,16,256]{2,1,0:T(8,128)(2,1)} %bitcast.10), calls=%async_computation.2 | async-start | bytes 1048576 | tf_op jit(solution)/shard_map/all_to_all | solution.py:74
  33.8 8.5 %copy-start.1 = (bf16[256,1024]{1,0:T(8,128)(2,1)S(1)}, bf16[256,1024]{1,0:T(8,128)(2,1)}, u32[]{:S(2)}) copy-start(bf16[256,1024]{1,0:T(8,128)(2,1)} %param.6) | copy-start | bytes 1572868
  35.0 8.2 %copy-start.2 = (bf16[256,1024]{1,0:T(8,128)(2,1)S(1)}, bf16[256,1024]{1,0:T(8,128)(2,1)}, u32[]{:S(2)}) copy-start(bf16[256,1024]{1,0:T(8,128)(2,1)} %param.7) | copy-start | bytes 1572868
  35.0 22.0 %all-to-all-start.3 = ((bf16[16,64,256]{2,0,1:T(8,128)(2,1)}), bf16[16,64,256]{2,0,1:T(8,128)(2,1)S(1)}, u32[]{:S(2)}, u32[]{:S(2)}) async-start(bf16[16,64,256]{2,0,1:T(8,128)(2,1)} %copy.35), calls=%async_computation.3 | async-start | bytes 1048576 | tf_op jit(solution)/shard_map/all_to_all | solution.py:91
  86.2 190.4 %all-to-all-start.1 = ((bf16[16,64,256]{2,0,1:T(8,128)(2,1)}), bf16[16,64,256]{2,0,1:T(8,128)(2,1)S(1)}, u32[]{:S(2)}, u32[]{:S(2)}) async-start(bf16[16,64,256]{2,0,1:T(8,128)(2,1)} %copy.32), calls=%async_computation.1 | async-start | bytes 1048576 | tf_op jit(solution)/shard_map/all_to_all | solution.py:90
where the time goes:
time: 279 us
  blocking collectives  198 us (71%)
  starting transfers between devices  28.2 us (10%)
  waiting for transfers between devices  27.3 us (10%)
  local copies, waits for them, and re-layouts  15.6 us (6%)
  matrix products  4.52 us (2%)
  other arithmetic  4.21 us (2%)
    all_gather x1, blocking collectives, shards(): raw_filters = lax.all_gather(partial_grad, 'ctx', axis=0, tiled=True)  128 us
    psum x1, blocking collectives, shards(): square_sum = lax.psum(jnp.sum(raw_filters * raw_filters), 'mp')  48.2 us
    all_to_all x1, blocking collectives, shards(): lax.all_to_all(product, 'ctx', split_axis=0, concat_axis=1, tiled=True)  21.8 us
    all_to_all x1, waiting for transfers between devices, shards(): lax.all_to_all(grad_mix, 'ctx', split_axis=0, concat_axis=1, tiled=True)  14.5 us
    all_to_all x1, starting transfers between devices, shards(): lax.all_to_all(grad_mix, 'ctx', split_axis=0, concat_axis=1, tiled=True)  12.9 us
    all_to_all x1, waiting for transfers between devices, shards(): lax.all_to_all(conv_grad, 'ctx', split_axis=1, concat_axis=0, tiled=True)  12.8 us
    unnamed x15, local copies, waits for them, and re-layouts  8.66 us
    all_to_all x1, starting transfers between devices, shards(): lax.all_to_all(conv_out, 'ctx', split_axis=1, concat_axis=0, tiled=True)  8.11 us
  transfers between devices with their start and end apart: 3, of which 2 were waited for; matrix products, arithmetic and copies ran while one was open for 3% of the time, Pallas kernels for 0%

commit v1 on v0

--- a/solution.py
+++ b/solution.py
@@ -89,7 +89,9 @@
     partial_grad = filter_grad(grad_rows, window_rows, filter_len)
     conv_rows = lax.all_to_all(conv_out, "ctx", split_axis=1, concat_axis=0, tiled=True)
     grad_back = lax.all_to_all(conv_grad, "ctx", split_axis=1, concat_axis=0, tiled=True)
-    raw_filters = lax.all_gather(partial_grad, "ctx", axis=0, tiled=True)
+    raw_filters = jnp.concatenate(
+        lax.all_to_all(jnp.stack([partial_grad] * lax.axis_size("ctx")), "ctx", 0, 0), axis=0
+    )
     conv_f = conv_rows.T.astype(jnp.float32)
     back_f = grad_back.T.astype(jnp.float32)
     mixer_out = (queries.astype(jnp.float32) * conv_f).astype(jnp.bfloat16)

time: 279 us -> 136 us (0.49)
  blocking collectives: 198 us -> 43.7 us
  starting transfers between devices: 28.2 us -> 33 us
  waiting for transfers between devices: 27.3 us -> 31.9 us
    all_gather x1 -> x0, blocking collectives: 128 us -> none  [shards(): raw_filters = lax.all_gather(partial_grad, 'ctx', axis=0, tiled=True)]
    psum x1, blocking collectives: 48.2 us -> 21.9 us  [shards(): square_sum = lax.psum(jnp.sum(raw_filters * raw_filters), 'mp')]
    all_to_all x0 -> x1, starting transfers between devices: none -> 8.1 us  [shards(): lax.all_to_all(jnp.stack([partial_grad] * lax.axis_size('ctx')), 'ctx', 0...]
    all_to_all x0 -> x1, waiting for transfers between devices: none -> 5.68 us  [shards(): lax.all_to_all(jnp.stack([partial_grad] * lax.axis_size('ctx')), 'ctx', 0...]
    all_to_all x1, starting transfers between devices: 8.11 us -> 4.98 us  [shards(): lax.all_to_all(conv_out, 'ctx', split_axis=1, concat_axis=0, tiled=True)]
  transfers between devices with their start and end apart: 3 -> 4, of which waited for: 2 -> 3; matrix products, arithmetic and copies ran while one was open for 3% -> 8% of each run, Pallas kernels for 0% -> 0%
where the time goes in v1:
time: 136 us; the launch traced here: 135 us
  blocking collectives  43.7 us (32%)
  starting transfers between devices  33 us (24%)
  waiting for transfers between devices  31.9 us (23%)
  local copies, waits for them, and re-layouts  17.3 us (13%)
  other arithmetic  4.21 us (3%)
  matrix products  3.36 us (2%)
  between operations  1.53 us (1%)
    psum x1, blocking collectives, shards(): square_sum = lax.psum(jnp.sum(raw_filters * raw_filters), 'mp')  21.9 us
    all_to_all x1, blocking collectives, shards(): lax.all_to_all(product, 'ctx', split_axis=0, concat_axis=1, tiled=True)  21.8 us
    all_to_all x1, waiting for transfers between devices, shards(): lax.all_to_all(grad_mix, 'ctx', split_axis=0, concat_axis=1, tiled=True)  14.5 us
    all_to_all x1, starting transfers between devices, shards(): lax.all_to_all(grad_mix, 'ctx', split_axis=0, concat_axis=1, tiled=True)  12.9 us
    all_to_all x1, waiting for transfers between devices, shards(): lax.all_to_all(conv_grad, 'ctx', split_axis=1, concat_axis=0, tiled=True)  11.8 us
    unnamed x15, local copies, waits for them, and re-layouts  9.7 us
    all_to_all x1, starting transfers between devices, shards(): lax.all_to_all(jnp.stack([partial_grad] * lax.axis_size('ctx')), 'ctx', 0...  8.1 us
    all_to_all x1, starting transfers between devices, shards(): lax.all_to_all(conv_grad, 'ctx', split_axis=1, concat_axis=0, tiled=True)  7.03 us
  transfers between devices with their start and end apart: 4, of which 3 were waited for; matrix products, arithmetic and copies ran while one was open for 8% of the time, Pallas kernels for 0%

profile of v1, /device:TPU:1, one launch (start us, length us, event | category | flops | bytes accessed | tf_op | source)
XLA Modules:
  0.0 135.1 jit_solution(17838911074544608488)
XLA Ops:
  0.6 0.0 copy-start
  0.6 1.2 copy.28
  1.9 1.2 copy.33
  3.1 0.9 fusion.6
  4.1 12.9 %all-to-all-start.2 = ((bf16[64,16,256]{2,1,0:T(8,128)(2,1)}), bf16[64,16,256]{2,1,0:T(8,128)(2,1)S(1)}, u32[]{:S(2)}, u32[]{:S(2)}) async-start(bf16[64,16,256]{2,1,0:T(8,128)(2,1)} %bitcast.10), calls=%async_computation.2 | async-start | bytes 1048576 | tf_op jit(solution)/shard_map/all_to_all | solution.py:74
  17.0 0.1 rev.8
  17.1 0.1 pad.6.clone
  17.2 0.1 fusion.13
  17.3 0.4 tile.13
  17.7 0.4 slice_reduce_fusion
  18.2 0.1 convolution_bitcast_fusion.2
  18.3 14.5 %all-to-all-done.2 = bf16[64,16,256]{2,1,0:T(8,128)(2,1)S(1)} async-done(((bf16[64,16,256]{2,1,0:T(8,128)(2,1)}), bf16[64,16,256]{2,1,0:T(8,128)(2,1)S(1)}, u32[]{:S(2)}, u32[]{:S(2)}) %all-to-all-start.2) | async-done | bytes 524320 | tf_op jit(solution)/shard_map/all_to_all | solution.py:74
  32.8 0.2 copy.34
  32.9 0.2 reshape.92
  33.1 0.4 convolution_bitcast_fusion
  33.5 0.1 slice.27
  33.6 0.1 fusion.9
  33.8 0.2 convert_element_type.93
  34.0 1.1 copy.35
  35.0 7.0 %all-to-all-start.3 = ((bf16[16,64,256]{2,0,1:T(8,128)(2,1)}), bf16[16,64,256]{2,0,1:T(8,128)(2,1)S(1)}, u32[]{:S(2)}, u32[]{:S(2)}) async-start(bf16[16,64,256]{2,0,1:T(8,128)(2,1)} %copy.35), calls=%async_computation.3 | async-start | bytes 1048576 | tf_op jit(solution)/shard_map/all_to_all | solution.py:91
  42.1 1.0 copy.29
  43.1 2.0 %copy.30 = bf16[256,1024]{0,1:T(8,128)(2,1)} copy(bf16[256,1024]{1,0:T(8,128)(2,1)} %param.7) | data formatting | bytes 1048576 | tf_op args[2]
  45.1 11.8 %all-to-all-done.3 = bf16[16,64,256]{2,0,1:T(8,128)(2,1)S(1)} async-done(((bf16[16,64,256]{2,0,1:T(8,128)(2,1)}), bf16[16,64,256]{2,0,1:T(8,128)(2,1)S(1)}, u32[]{:S(2)}, u32[]{:S(2)}) %all-to-all-start.3) | async-done | bytes 524320 | tf_op jit(solution)/shard_map/all_to_all | solution.py:91
  56.9 1.5 %fusion.2 = (bf16[256,1024]{0,1:T(8,128)(2,1)S(1)}, bf16[256,1024]{0,1:T(8,128)(2,1)S(1)}, bf16[256,1024]{0,1:T(8,128)(2,1)S(1)}) fusion(bf16[256,1024]{0,1:T(8,128)(2,1)} %copy.29, bf16[16,64,256]{2,0,1:T(8,128)(2,1)S(1)} %all-to-all-done.3, bf16[256,1024]{0,1:T(8,128)(2,1)} %copy.30), kind=kLoop, calls=%fused_computation.13 | loop fusion | flops 2359296 | bytes 3145728 | tf_op jit(solution)/shard_map/convert_element_type | solution.py:100
  58.4 21.8 %all_to_all.57 = bf16[64,16,256]{2,1,0:T(8,128)(2,1)S(1)} all-to-all(bf16[64,16,256]{2,1,0:T(8,128)(2,1)S(1)} %bitcast.50), channel_id=1, replica_groups=mesh['ctx'=64,'mp'=8] {'ctx'}, dimensions={0} | all-to-all | bytes 1048576 | tf_op jit(solution)/shard_map/all_to_all | solution.py:73
  80.2 0.2 copy.31
  80.4 1.0 reshape_reshape.2
  81.4 1.6 %convolution_bitcast_fusion.1 = f32[1,1,128,256]{3,2,1,0:T(8,128)S(1)} fusion(bf16[16,128,128]{2,1,0:T(8,128)(2,1)S(1)} %reshape.92, bf16[1,16,127,128]{3,2,1,0:T(8,128)(2,1)} %bitcast.51, bf16[1,16,128,128]{3,2,1,0:T(8,128)(2,1)} %reshape_reshape.2), kind=kOutput, calls=%fused_computation.10 | convolution fusion | flops 137363456 | bytes 1699840 | tf_op jit(solution)/shard_map/gsna,gsnm->gam/dot_general | solution.py:11
  83.0 0.1 copy.42
  83.1 0.3 pad_reduce_fusion
  83.4 0.3 reshape.94
  83.8 0.1 slice.29
  83.9 0.1 rev.9
  84.0 0.6 stack.2
  84.6 8.1 %all-to-all-start.4 = ((f32[64,1,128]{2,1,0:T(1,128)}), f32[64,1,128]{2,1,0:T(1,128)S(1)}, u32[]{:S(2)}, u32[]{:S(2)}) async-start(f32[64,1,128]{2,1,0:T(1,128)} %stack.2), calls=%async_computation.4 | async-start | bytes 65536 | tf_op jit(solution)/shard_map/all_to_all | solution.py:93
  92.8 1.2 convolution_convert_fusion
  94.0 1.2 convert_element_type.83
  95.2 1.1 copy.32
  96.3 5.7 %all-to-all-done.4 = f32[64,1,128]{2,1,0:T(1,128)S(1)} async-done(((f32[64,1,128]{2,1,0:T(1,128)}), f32[64,1,128]{2,1,0:T(1,128)S(1)}, u32[]{:S(2)}, u32[]{:S(2)}) %all-to-all-start.4) | async-done | bytes 32800 | tf_op jit(solution)/shard_map/all_to_all | solution.py:93
  102.0 5.0 %all-to-all-start.1 = ((bf16[16,64,256]{2,0,1:T(8,128)(2,1)}), bf16[16,64,256]{2,0,1:T(8,128)(2,1)S(1)}, u32[]{:S(2)}, u32[]{:S(2)}) async-start(bf16[16,64,256]{2,0,1:T(8,128)(2,1)} %copy.32), calls=%async_computation.1 | async-start | bytes 1048576 | tf_op jit(solution)/shard_map/all_to_all | solution.py:90
  107.0 1.0 copy.39
  108.0 0.7 multiply_reduce_fusion
  108.6 1.0 copy.40
  109.6 21.9 %psum.7 = f32[]{:T(128)} all-reduce(f32[]{:T(128)} %multiply_reduce_fusion), channel_id=1, replica_groups=mesh['ctx'=64,'mp'=8] {'mp'}, use_global_device_ids=true, to_apply=%region_2.0 | all-reduce | flops 1 | bytes 8 | tf_op jit(solution)/shard_map/psum | solution.py:101
  132.2 0.6 broadcast_multiply_fusion
  132.8 0.2 fusion.5
  133.1 1.0 copy.37
  134.1 1.0 copy.38
  (14 shorter events, 0.1 us)
Async XLA Ops:
  0.6 16.4 %copy-start = (bf16[64,128]{1,0:T(8,128)(2,1)S(1)}, bf16[64,128]{1,0:T(8,128)(2,1)}, u32[]{:S(2)}) copy-start(bf16[64,128]{1,0:T(8,128)(2,1)} %param.8) | copy-start | bytes 49156
  4.1 28.7 %all-to-all-start.2 = ((bf16[64,16,256]{2,1,0:T(8,128)(2,1)}), bf16[64,16,256]{2,1,0:T(8,128)(2,1)S(1)}, u32[]{:S(2)}, u32[]{:S(2)}) async-start(bf16[64,16,256]{2,1,0:T(8,128)(2,1)} %bitcast.10), calls=%async_computation.2 | async-start | bytes 1048576 | tf_op jit(solution)/shard_map/all_to_all | solution.py:74
  33.9 8.1 %copy-start.1 = (bf16[256,1024]{1,0:T(8,128)(2,1)S(1)}, bf16[256,1024]{1,0:T(8,128)(2,1)}, u32[]{:S(2)}) copy-start(bf16[256,1024]{1,0:T(8,128)(2,1)} %param.6) | copy-start | bytes 1572868
  35.0 21.8 %all-to-all-start.3 = ((bf16[16,64,256]{2,0,1:T(8,128)(2,1)}), bf16[16,64,256]{2,0,1:T(8,128)(2,1)S(1)}, u32[]{:S(2)}, u32[]{:S(2)}) async-start(bf16[16,64,256]{2,0,1:T(8,128)(2,1)} %copy.35), calls=%async_computation.3 | async-start | bytes 1048576 | tf_op jit(solution)/shard_map/all_to_all | solution.py:91
  81.4 11.4 %copy-start.2 = (bf16[1,16,128,128]{3,2,1,0:T(8,128)(2,1)S(1)}, bf16[1,16,128,128]{3,2,1,0:T(8,128)(2,1)}, u32[]{:S(2)}) copy-start(bf16[1,16,128,128]{3,2,1,0:T(8,128)(2,1)} %reshape_reshape.2) | copy-start | bytes 1572868
  84.6 17.3 %all-to-all-start.4 = ((f32[64,1,128]{2,1,0:T(1,128)}), f32[64,1,128]{2,1,0:T(1,128)S(1)}, u32[]{:S(2)}, u32[]{:S(2)}) async-start(f32[64,1,128]{2,1,0:T(1,128)} %stack.2), calls=%async_computation.4 | async-start | bytes 65536 | tf_op jit(solution)/shard_map/all_to_all | solution.py:93
  102.0 30.8 %all-to-all-start.1 = ((bf16[16,64,256]{2,0,1:T(8,128)(2,1)}), bf16[16,64,256]{2,0,1:T(8,128)(2,1)S(1)}, u32[]{:S(2)}, u32[]{:S(2)}) async-start(bf16[16,64,256]{2,0,1:T(8,128)(2,1)} %copy.32), calls=%async_computation.1 | async-start | bytes 1048576 | tf_op jit(solution)/shard_map/all_to_all | solution.py:90
